TPU v7x, 32 devices: a whole 2x2x4 slice. The times are simulated.
32 devices in a mesh: group: 2 (over x), seq: 4 (over y, core), fsdp: 4 (over z).
Axes of the slice: x: 2, y: 2, z: 4, core: 2. Of those that a mesh axis runs over, the one named last changes fastest.
Arguments:
- latents: bfloat16 [8192, 3072], P(('group', 'seq', 'fsdp')), parts along dimension 0, may hold values from -6 to 6
- qkv_weight: bfloat16 [3072, 3, 3072], P('seq', None, 'fsdp'), may hold values from -0.109375 to 0.109375
- out_weight: bfloat16 [3072, 3072], P('fsdp', 'seq'), may hold values from -0.109375 to 0.109375
- mod_weight: bfloat16 [256, 3, 3072], P(None, None, ('seq', 'fsdp')), may hold values from -1 to 1
- q_gain: float32 [128], replicated, may hold values from 0.5 to 12, as said below
- k_gain: float32 [128], replicated, may hold values from 0.5 to 12, as said below
- tile_slot: int32 [8, 16], P('group'), parts along dimension 0, may hold values from 0 to 15, each once within a row
- win_start: int32 [8, 16, 3], P('group'), parts along dimension 0, may hold values from 0 to 2, as said below
- step_index: int32 [2], P('group'), parts along dimension 0, may hold values from 0 to 999
Outputs:
- updated: bfloat16 [8192, 3072], P(('group', 'seq', 'fsdp')), parts along dimension 0
There are 2 independent parts, one for each index of `group`. A program takes and returns all parts, laid end to end along the dimension named above; an argument that names none is the same for every part. Nothing has to cross between parts.
Inputs may be any that keep to these rules, and one draw needn't show every extreme that they name: win_start[t, p] holds the first time slice, tile row and tile column of the window of the tile at spatial position p (row p // 4, column p % 4) of slice t; the window spans 2 slices, 3 rows and 3 columns inside the clip and contains the tile itself. `tile_slot`: each row is an ordering of the 16 spatial tiles. `q_gain`: positive gains. `k_gain`: positive gains.
All inputs are finite; a program needn't handle non-finite values.
Results may differ from a plain program's by a relative error of at most 0.014.
The roundings to bfloat16 on the way count: a program that leaves them out, or rounds other values in their place, can miss the bound.
Values may be sent and summed in bfloat16 or wider, within the bound.
A program may use at most 192 MiB of HBM per device.

v0:
```python
import math

import jax
import jax.numpy as jnp
from jax import lax
from jax.sharding import PartitionSpec as P

HD = 128
FREQ = 256
TILE = 64
GW = 4


def with_halo(block, sides, width):
    for axis, dim in sides:
        count = lax.axis_size(axis)
        forward = [(i, i + 1) for i in range(count - 1)]
        backward = [(target, source) for source, target in forward]
        low = lax.ppermute(
            lax.slice_in_dim(block, block.shape[dim] - width, None, axis=dim), axis, forward
        )
        high = lax.ppermute(lax.slice_in_dim(block, 0, width, axis=dim), axis, backward)
        block = jnp.concatenate([low, block, high], axis=dim)
    return block


def time_signal(step_index):
    halfway = FREQ // 2
    freqs_all = jnp.exp(-math.log(10000.0) * jnp.arange(halfway, dtype=jnp.float32) / halfway)
    angles = step_index[0].astype(jnp.float32) * freqs_all
    return jax.nn.silu(jnp.concatenate([jnp.cos(angles), jnp.sin(angles)])).astype(jnp.bfloat16)


def modulate(tokens_in, shift_mod, scale_mod):
    values = tokens_in.astype(jnp.float32)
    centre = jnp.mean(values, axis=-1, keepdims=True)
    spread = jnp.mean((values - centre) ** 2, axis=-1, keepdims=True)
    normal = (values - centre) * lax.rsqrt(spread + 1e-06)
    return (normal * (1.0 + scale_mod) + shift_mod).astype(jnp.bfloat16)


def rms_scale(values, gain_vec):
    return values * lax.rsqrt(jnp.mean(values * values, axis=-1, keepdims=True) + 1e-06) * gain_vec


def project_rows(normed, weight_flat, q_gain, k_gain):
    mixture = jnp.dot(normed, weight_flat, preferred_element_type=jnp.float32)
    row_count = normed.shape[0]
    mixture = mixture.reshape(row_count, 3, -1, HD)
    queries = rms_scale(mixture[:, 0], q_gain)
    key_vecs = rms_scale(mixture[:, 1], k_gain)
    return (
        jnp.stack([queries, key_vecs, mixture[:, 2]], axis=1)
        .reshape(row_count, -1)
        .astype(jnp.bfloat16)
    )


def slot_masks(tile_slot, win_start, block_idx):
    blocks_total = tile_slot.shape[0]
    spot_count = tile_slot.shape[1]
    ids_query = lax.dynamic_index_in_dim(tile_slot, block_idx, 0, keepdims=False)
    window_row = lax.dynamic_index_in_dim(win_start, block_idx, 0, keepdims=False)
    onehot = ids_query[:, None] == jnp.arange(spot_count, dtype=jnp.int32)[None, :]
    corner = jnp.sum(jnp.where(onehot[:, :, None], window_row[None], 0), axis=1)
    result = []
    for offset in (-1, 0, 1):
        key_time = block_idx + offset
        ids_key = lax.dynamic_index_in_dim(
            tile_slot, jnp.clip(key_time, 0, blocks_total - 1), 0, keepdims=False
        )
        tile_row = ids_key // GW
        tile_col = ids_key % GW
        inside = (corner[:, 0:1] <= key_time) & (key_time <= corner[:, 0:1] + 1)
        inside = (
            inside & (corner[:, 1:2] <= tile_row[None]) & (tile_row[None] <= corner[:, 1:2] + 2)
        )
        inside = (
            inside & (corner[:, 2:3] <= tile_col[None]) & (tile_col[None] <= corner[:, 2:3] + 2)
        )
        result.append(jnp.repeat(jnp.repeat(inside, TILE, axis=0), TILE, axis=1))
    return result


def body(
    latents, qkv_weight, out_weight, mod_weight, q_gain, k_gain, tile_slot, win_start, step_index
):
    signal = time_signal(step_index)
    local_cols = mod_weight.shape[2]
    own_mod = jnp.dot(
        signal[None], mod_weight.reshape(FREQ, 3 * local_cols), preferred_element_type=jnp.float32
    ).reshape(3, local_cols)
    modulation = lax.all_gather(own_mod, ("seq", "fsdp"), axis=1, tiled=True)
    shift_mod = modulation[0]
    scale_mod = modulation[1]
    gate_mod = modulation[2]
    qkv_full = lax.all_gather(qkv_weight, "seq", axis=0, tiled=True)
    out_full = lax.all_gather(out_weight, "seq", axis=1, tiled=True)
    model_width = qkv_full.shape[0]
    group_width = qkv_full.shape[2]
    head_count = group_width // HD
    weight_flat = qkv_full.reshape(model_width, 3 * group_width)
    packed = project_rows(
        modulate(lax.all_gather(latents, "fsdp", axis=0, tiled=True), shift_mod, scale_mod),
        weight_flat,
        q_gain,
        k_gain,
    )
    block_tokens = packed.shape[0]
    query_all = packed[:, :group_width].reshape(block_tokens, head_count, HD)
    kv_local = packed[:, group_width:]
    extended = with_halo(kv_local[None], (("seq", 0),), 1)
    key_all = extended[:, :, :group_width].reshape(3, block_tokens, head_count, HD)
    value_all = extended[:, :, group_width:].reshape(3, block_tokens, head_count, HD)
    visible = slot_masks(tile_slot, win_start, lax.axis_index("seq"))
    inv_root = 1.0 / math.sqrt(HD)
    query_span = 512
    head_outputs = []
    for head_idx in range(head_count):
        row_parts = []
        for query_blk in range(block_tokens // query_span):
            lower = query_blk * query_span
            queries = query_all[lower : lower + query_span, head_idx]
            running_top = jnp.full((query_span,), -1e30, jnp.float32)
            running_total = jnp.zeros((query_span,), jnp.float32)
            accum = jnp.zeros((query_span, HD), jnp.float32)
            for key_blk in range(3):
                scores = (
                    lax.dot_general(
                        queries,
                        key_all[key_blk, :, head_idx],
                        (((1,), (1,)), ((), ())),
                        preferred_element_type=jnp.float32,
                    )
                    * inv_root
                )
                allowed = visible[key_blk][lower : lower + query_span]
                shifted = jnp.where(allowed, scores, -1e30)
                new_top = jnp.maximum(running_top, jnp.max(shifted, axis=1))
                weights = jnp.where(allowed, jnp.exp(shifted - new_top[:, None]), 0.0)
                factor = jnp.exp(running_top - new_top)
                running_total = running_total * factor + jnp.sum(weights, axis=1)
                accum = accum * factor[:, None] + jnp.dot(
                    weights.astype(jnp.bfloat16),
                    value_all[key_blk, :, head_idx],
                    preferred_element_type=jnp.float32,
                )
                running_top = new_top
            row_parts.append(accum / running_total[:, None])
        head_outputs.append(jnp.concatenate(row_parts, axis=0))
    attended = (
        jnp.stack(head_outputs, axis=1).reshape(block_tokens, group_width).astype(jnp.bfloat16)
    )
    projected = lax.psum_scatter(
        jnp.dot(attended, out_full, preferred_element_type=jnp.float32).astype(jnp.bfloat16),
        "fsdp",
        scatter_dimension=0,
        tiled=True,
    ).astype(jnp.float32)
    return (latents.astype(jnp.float32) + gate_mod * projected).astype(jnp.bfloat16)


def solution(mesh):
    in_specs = (
        P(("group", "seq", "fsdp"), None),
        P("seq", None, "fsdp"),
        P("fsdp", "seq"),
        P(None, None, ("seq", "fsdp")),
        P(),
        P(),
        P("group", None),
        P("group", None, None),
        P("group"),
    )
    out_specs = P(("group", "seq", "fsdp"), None)
    return jax.shard_map(body, mesh=mesh, in_specs=in_specs, out_specs=out_specs, check_vma=False)
```

profile of v0, /device:TPU:9, one launch (start us, length us, event | category | flops | bytes accessed | tf_op | source)
XLA Modules:
  0.0 622.7 jit_solution(11329790541286253678)
XLA Ops:
  7.3 6.1 copy.163
  14.4 31.8 %all-gather = f32[16,192,3]{1,2,0:T(4,128)S(1)} all-gather(f32[1,192,3]{1,2,0:T(4,128)S(1)} %bitcast.464), channel_id=1, replica_groups=mesh['group'=2,'seq'=4,'fsdp'=4] {'seq','fsdp'}, dimensions={0}, use_global_device_ids=true | all-gather | bytes 39168 | tf_op jit(solution)/shard_map/all_gather | solution.py:93
  46.9 76.9 %all-gather.5.cloned.1.call-done = bf16[1024,3072]{1,0:T(8,128)(2,1)} async-done(((bf16[256,3072]{1,0:T(8,128)(2,1)}), bf16[1024,3072]{1,0:T(8,128)(2,1)}) %all-gather.5.cloned.1.call-update) | async-done | bytes 6291472 | tf_op jit(solution)/shard_map/all_gather | solution.py:104
  123.8 3.8 convert_reduce_fusion
  130.2 87.7 %all-gather.7.cloned.1.call-done = bf16[3072,3,768]{0,2,1:T(8,128)(2,1)} async-done(((bf16[768,3,768]{0,2,1:T(8,128)(2,1)}), bf16[3072,3,768]{0,2,1:T(8,128)(2,1)}) %all-gather.7.cloned.1.call-update) | async-done | bytes 14155792 | tf_op jit(solution)/shard_map/all_gather | solution.py:97
  217.8 20.0 %fusion.7 = f32[1024,3,6,128]{0,3,2,1:T(8,128)S(1)} fusion(bf16[3,6,128,3072]{3,2,1,0:T(8,128)(2,1)} %bitcast.468, bf16[1024,3072]{1,0:T(8,128)(2,1)} %all-gather.5.cloned.1.call-done, f32[3072]{0:T(1024)S(1)} %bitcast.465, f32[3072]{0:T(1024)S(1)} %bitcast.466, f32[1024]{0:T(1024)S(1)} %add_rsqrt_fusion.2, f32[1024]{0:T(1024)S(1)} %broadcast_multiply_fusion), kind=kOutput, calls=%fused_computation.10 | convolution fusion | flops 14514388992 | bytes 29917184 | tf_op jit(solution)/shard_map/dot_general | solution.py:47
  243.3 2.3 collective-permute-start
  245.6 3.8 collective-permute-start.1
  263.4 41.7 %collective-permute-done = bf16[1,1024,1536]{1,2,0:T(8,128)(2,1)} collective-permute-done((bf16[1,1024,1536]{1,2,0:T(8,128)(2,1)S(1)}, bf16[1,1024,1536]{1,2,0:T(8,128)(2,1)}, u32[]{:S(2)}, u32[]{:S(2)}) %collective-permute-start) | collective-permute-done | bytes 3145760 | tf_op jit(solution)/shard_map/ppermute | solution.py:19
  305.0 4.5 collective-permute-done.1
  309.5 7.7 %pad_maximum_fusion = bf16[3,1024,1536]{1,2,0:T(8,128)(2,1)} fusion(bf16[1,1024,1536]{1,2,0:T(8,128)(2,1)} %collective-permute-done.1, bf16[1,1024,1536]{1,2,0:T(8,128)(2,1)S(1)} %slice_bitcast_fusion, bf16[1,1024,1536]{1,2,0:T(8,128)(2,1)} %collective-permute-done), kind=kLoop, calls=%fused_computation.8 | loop fusion | flops 9437184 | bytes 18874368 | tf_op jit(solution)/shard_map/concatenate | solution.py:23
  317.2 7.1 %fusion.406 = (bf16[3,1024,768]{1,2,0:T(8,128)(2,1)}, bf16[3,1024,768]{1,2,0:T(8,128)(2,1)S(1)}) fusion(bf16[3,1024,1536]{1,2,0:T(8,128)(2,1)} %pad_maximum_fusion), kind=kLoop, calls=%fused_computation.634 | loop fusion | bytes 18874368 | tf_op jit(solution)/shard_map/slice | solution.py:114
  337.4 2.0 fusion.227
  359.8 5.0 fusion.43
  364.8 5.1 fusion.44
  369.9 4.7 fusion.45
  374.7 10.0 %fusion.109 = (f32[512]{0:T(512)S(1)}, f32[512]{0:T(512)S(1)}, f32[512]{0:T(512)S(1)}, f32[512]{0:T(512)S(1)}, f32[512]{0:T(512)S(1)}, /*index=5*/f32[512]{0:T(512)S(1)}) fusion(pred[512,1024]{1,0:T(32,128)(4,1)} %copy.164, f32[512,1024]{1,0:T(8,128)} %get-tuple-element.202, f32[512]{0:T(512)S(1)} %get-tuple-element.167, f32[512]{0:T(512)S(1)} %get-tuple-element.166, ...), kind=kLoop, calls=%fused_computation.192 | loop fusion | flops 15725568 | bytes 13131776 | tf_op jit(solution)/shard_map/reduce_sum | solution.py:142
  384.7 6.6 %fusion.111 = (f32[512]{0:T(512)S(1)}, f32[512]{0:T(512)S(1)}, f32[512]{0:T(512)S(1)}, f32[512]{0:T(512)S(1)}, f32[512]{0:T(512)S(1)}, /*index=5*/f32[512]{0:T(512)S(1)}) fusion(pred[512,1024]{1,0:T(32,128)(4,1)S(1)} %copy-done.28, f32[512,1024]{1,0:T(8,128)} %get-tuple-element.201, f32[512]{0:T(512)S(1)} %get-tuple-element.121, ...), kind=kLoop, calls=%fused_computation.194 | loop fusion | flops 15725568 | bytes 13131776 | tf_op jit(solution)/shard_map/reduce_sum | solution.py:142
  391.3 6.6 %fusion.113 = (f32[512]{0:T(512)S(1)}, f32[512]{0:T(512)S(1)}, f32[512]{0:T(512)S(1)}, f32[512]{0:T(512)S(1)}, f32[512]{0:T(512)S(1)}, /*index=5*/f32[512]{0:T(512)S(1)}) fusion(pred[512,1024]{1,0:T(32,128)(4,1)S(1)} %copy-done.29, f32[512,1024]{1,0:T(8,128)} %get-tuple-element.200, f32[512]{0:T(512)S(1)} %get-tuple-element.120, ...), kind=kLoop, calls=%fused_computation.196 | loop fusion | flops 15725568 | bytes 13131776 | tf_op jit(solution)/shard_map/reduce_sum | solution.py:142
  398.0 2.9 fusion.144
  404.5 5.3 fusion.46
  409.9 4.7 fusion.47
  414.6 4.7 fusion.48
  419.3 10.2 %fusion.115 = (f32[512]{0:T(512)S(1)}, f32[512]{0:T(512)S(1)}, f32[512]{0:T(512)S(1)}, f32[512]{0:T(512)S(1)}, f32[512]{0:T(512)S(1)}, /*index=5*/f32[512]{0:T(512)S(1)}) fusion(pred[512,1024]{1,0:T(32,128)(4,1)} %copy.170, f32[512,1024]{1,0:T(8,128)} %get-tuple-element.199, f32[512]{0:T(512)S(1)} %get-tuple-element.180, f32[512]{0:T(512)S(1)} %get-tuple-element.179, ...), kind=kLoop, calls=%fused_computation.198 | loop fusion | flops 15725568 | bytes 13131776 | tf_op jit(solution)/shard_map/reduce_sum | solution.py:142
  429.6 9.3 %fusion.117 = (f32[512]{0:T(512)S(1)}, f32[512]{0:T(512)S(1)}, f32[512]{0:T(512)S(1)}, f32[512]{0:T(512)S(1)}, f32[512]{0:T(512)S(1)}, /*index=5*/f32[512]{0:T(512)S(1)}) fusion(pred[512,1024]{1,0:T(32,128)(4,1)} %copy.172, f32[512,1024]{1,0:T(8,128)} %get-tuple-element.198, f32[512]{0:T(512)S(1)} %get-tuple-element.136, f32[512]{0:T(512)S(1)} %get-tuple-element.134, ...), kind=kLoop, calls=%fused_computation.200 | loop fusion | flops 15725568 | bytes 13131776 | tf_op jit(solution)/shard_map/reduce_sum | solution.py:142
  438.9 9.5 %fusion.119 = (f32[512]{0:T(512)S(1)}, f32[512]{0:T(512)S(1)}, f32[512]{0:T(512)S(1)}, f32[512]{0:T(512)S(1)}, f32[512]{0:T(512)S(1)}, /*index=5*/f32[512]{0:T(512)S(1)}) fusion(pred[512,1024]{1,0:T(32,128)(4,1)} %copy.174, f32[512,1024]{1,0:T(8,128)} %get-tuple-element.197, f32[512]{0:T(512)S(1)} %get-tuple-element.135, f32[512]{0:T(512)S(1)} %get-tuple-element.133, ...), kind=kLoop, calls=%fused_computation.202 | loop fusion | flops 15725568 | bytes 13131776 | tf_op jit(solution)/shard_map/reduce_sum | solution.py:142
  448.4 2.9 fusion.141
  453.2 1.8 fusion.162
  458.9 1.8 fusion.159
  492.9 9.4 %convolution_convert_fusion = bf16[1024,3072]{1,0:T(8,128)(2,1)} fusion(bf16[1024,768]{0,1:T(8,128)(2,1)S(1)} %bitcast.461, bf16[768,3072]{1,0:T(8,128)(2,1)} %all-gather.9.cloned.1.call-done), kind=kOutput, calls=%fused_computation.15 | convolution fusion | flops 4834983936 | bytes 12582912 | tf_op jit(solution)/shard_map/dot_general | solution.py:155
  502.3 110.4 %reduce-scatter.2.cloned.1.call-done = bf16[256,3072]{1,0:T(8,128)(2,1)} async-done(((bf16[1024,3072]{1,0:T(8,128)(2,1)}), bf16[256,3072]{1,0:T(8,128)(2,1)}) %reduce-scatter.2.cloned.1.call-update) | async-done | bytes 1572880 | tf_op jit(solution)/shard_map/reduce_scatter | solution.py:154
  612.8 3.2 add_convert_fusion
  (246 shorter events, 98.0 us)
Async XLA Ops:
  6.5 7.6 %copy-start = (bf16[256,3,192]{0,2,1:T(8,128)(2,1)S(1)}, bf16[256,3,192]{0,2,1:T(8,128)(2,1)}, u32[]{:S(2)}) copy-start(bf16[256,3,192]{0,2,1:T(8,128)(2,1)} %param.12) | copy-start | bytes 884740
  6.5 117.3 %all-gather.5.cloned.1.call-start = ((), (), s32[]{:S(2)}) async-start(), calls=%async_computation.1 | async-start | bytes 7864320 | tf_op jit(solution)/shard_map/all_gather | solution.py:104
  7.3 210.6 %all-gather.7.cloned.1.call-start = ((), (), s32[]{:S(2)}) async-start(), calls=%async_computation.2 | async-start | bytes 17694720 | tf_op jit(solution)/shard_map/all_gather | solution.py:97
  13.4 479.5 %all-gather.9.cloned.1.call-start = ((), (), s32[]{:S(2)}) async-start(), calls=%async_computation.3 | async-start | bytes 5898240 | tf_op jit(solution)/shard_map/all_gather | solution.py:98
  123.8 4.6 copy-start.2
  241.2 2.1 copy-start.3
  241.2 9.4 %copy-start.39 = (s32[4,16]{1,0:T(4,128)S(1)}, s32[4,16]{1,0:T(4,128)}, u32[]{:S(2)}) copy-start(s32[4,16]{1,0:T(4,128)} %param.15) | copy-start | bytes 772
  243.3 61.8 %collective-permute-start = (bf16[1,1024,1536]{1,2,0:T(8,128)(2,1)S(1)}, bf16[1,1024,1536]{1,2,0:T(8,128)(2,1)}, u32[]{:S(2)}, u32[]{:S(2)}) collective-permute-start(bf16[1,1024,1536]{1,2,0:T(8,128)(2,1)S(1)} %slice_bitcast_fusion), channel_id=1, source_target_pairs={{0,4},{4,8},{8,12},{1,5},{5,9},{9,13},{2,6},{6,10},{10,14},{3,7},{... | collective-permute-start | bytes 9437192 | tf_op jit(solution)/shard_map/ppermute | solution.py:19
  245.6 64.0 %collective-permute-start.1 = (bf16[1,1024,1536]{1,2,0:T(8,128)(2,1)S(1)}, bf16[1,1024,1536]{1,2,0:T(8,128)(2,1)}, u32[]{:S(2)}, u32[]{:S(2)}) collective-permute-start(bf16[1,1024,1536]{1,2,0:T(8,128)(2,1)S(1)} %slice_bitcast_fusion), channel_id=1, source_target_pairs={{4,0},{8,4},{12,8},{5,1},{9,5},{13,9},{6,2},{10,6},{14,10},{7,3},{... | collective-permute-start | bytes 9437192 | tf_op jit(solution)/shard_map/ppermute | solution.py:22
  249.4 363.4 %reduce-scatter.2.cloned.1.call-start = ((), (), s32[]{:S(2)}) async-start(), calls=%async_computation.4 | async-start | bytes 7864320 | tf_op jit(solution)/shard_map/reduce_scatter | solution.py:154
  337.4 32.6 %copy-start.7 = (f32[512,1024]{1,0:T(8,128)}, f32[512,1024]{1,0:T(8,128)S(1)}, u32[]{:S(2)}) copy-start(f32[512,1024]{1,0:T(8,128)S(1)} %fusion.221) | copy-start | bytes 6291460
  359.8 5.0 copy-start.28
  364.8 5.1 copy-start.29
  398.0 2.9 copy-start.20
  404.5 5.4 copy-start.4
  404.5 5.3 copy-start.34
  409.8 4.7 copy-start.32
  419.3 10.2 %copy-start.5 = (f32[512,1024]{1,0:T(8,128)S(1)}, f32[512,1024]{1,0:T(8,128)}, u32[]{:S(2)}) copy-start(f32[512,1024]{1,0:T(8,128)} %fusion.218) | copy-start | bytes 6291460
  419.3 10.2 %copy-start.13 = (f32[512,1024]{1,0:T(8,128)S(1)}, f32[512,1024]{1,0:T(8,128)}, u32[]{:S(2)}) copy-start(f32[512,1024]{1,0:T(8,128)} %fusion.224) | copy-start | bytes 6291460
  429.6 9.3 %copy-start.12 = (f32[512,1024]{1,0:T(8,128)S(1)}, f32[512,1024]{1,0:T(8,128)}, u32[]{:S(2)}) copy-start(f32[512,1024]{1,0:T(8,128)} %fusion.226) | copy-start | bytes 6291460
  448.4 2.9 copy-start.18
  448.4 2.9 copy-start.35
  451.4 1.9 copy-start.17
  453.2 1.9 copy-start.15
  453.2 1.9 copy-start.31
  458.8 1.9 copy-start.11
  458.8 1.9 copy-start.37
  458.9 5.4 slice-start
  460.8 3.5 slice-start.1
  502.3 110.5 %copy-start.27 = (bf16[256,3072]{1,0:T(8,128)(2,1)S(1)}, bf16[256,3072]{1,0:T(8,128)(2,1)}, u32[]{:S(2)}) copy-start(bf16[256,3072]{1,0:T(8,128)(2,1)} %param.9) | copy-start | bytes 4718596
  502.3 110.5 %copy-start.38 = (f32[1,3072]{1,0:T(1,128)S(1)}, f32[1,3072]{1,0:T(1,128)}, u32[]{:S(2)}) copy-start(f32[1,3072]{1,0:T(1,128)} %get-tuple-element.149) | copy-start | bytes 36868
  612.8 3.2 copy-start.1
  (18 other events, 27.4 us)
Sparse Core Ops, SparseCore 0:
  8.9 114.8 all-gather.4
  125.4 92.4 all-gather.6
  249.5 50.0 all-gather.8
  502.5 110.2 reduce-scatter.1
where the time goes:
time: 633 us; the launch traced here: 623 us
  waiting for transfers between devices  322 us (51%)
  matrix products  135 us (21%)
  other arithmetic  72.8 us (12%)
  local copies, waits for them, and re-layouts  39 us (6%)
  blocking collectives  31.8 us (5%)
  between operations  15.2 us (2%)
  starting transfers between devices  6.66 us (1%)
    reduce_scatter x1, waiting for transfers between devices, body(): lax.psum_scatter(jnp.dot(attended, out_full, preferred_element_type=jnp.f...  110 us
    all_gather x1, waiting for transfers between devices, body(): qkv_full = lax.all_gather(qkv_weight, 'seq', axis=0, tiled=True)  87.7 us
    all_gather x1, waiting for transfers between devices, body(): lax.all_gather(latents, 'fsdp', axis=0, tiled=True)  76.9 us
    dot_general x36, matrix products, body(): lax.dot_general(queries, key_all[key_blk, :, head_idx], (((1,), (1,)), ((...  64.8 us
    reduce_sum x6, other arithmetic, body(): running_total = running_total * factor + jnp.sum(weights, axis=1)  52.2 us
    ppermute x1, waiting for transfers between devices, with_halo(): lax.ppermute(lax.slice_in_dim(block, block.shape[dim] - width, None, axis...  41.7 us
    dot_general x36, matrix products, body(): jnp.dot(weights.astype(jnp.bfloat16), value_all[key_blk, :, head_idx], pr...  40.8 us
    all_gather x1, blocking collectives, body(): modulation = lax.all_gather(own_mod, ('seq', 'fsdp'), axis=1, tiled=True)  31.8 us
  transfers between devices with their start and end apart: 6, of which 5 were waited for; matrix products, arithmetic and copies ran while one was open for 32% of the time, Pallas kernels for 0%

commit v1 on v0

--- a/solution.py
+++ b/solution.py
@@ -1,8 +1,11 @@
+import functools
 import math
 
 import jax
 import jax.numpy as jnp
 from jax import lax
+from jax.experimental import pallas as pl
+from jax.experimental.pallas import tpu as pltpu
 from jax.sharding import PartitionSpec as P
 
 HD = 128
@@ -159,6 +162,410 @@
     ).astype(jnp.float32)
     return (latents.astype(jnp.float32) + gate_mod * projected).astype(jnp.bfloat16)
 
+MESH = pl.DeviceIdType.MESH
+BF = jnp.bfloat16
+F32 = jnp.float32
+VMEM_LIMIT = 62 * 1024 * 1024
+
+
+def entry_barrier(peers):
+    barrier = pltpu.get_barrier_semaphore()
+    for peer in peers:
+        pl.semaphore_signal(barrier, inc=1, device_id=peer, device_id_type=MESH)
+    pl.semaphore_wait(barrier, len(peers))
+
+
+def gather_kernel(
+    lat_ref, w_ref, ow_ref, mod_ref, qg_ref, kg_ref,
+    q_out, kv_out, ow_all, mod_out,
+    lat_all, w_all, mod_all, nrm,
+    loc_sem, mod_s, mod_r, lat_s, lat_r, w_s, w_r, ow_s, ow_r, kv_s, kv_r,
+):
+    s = lax.axis_index("seq")
+    z = lax.axis_index("fsdp")
+    me = s * 4 + z
+    rows = lat_ref.shape[0]
+    yp = lax.rem(s + 2, 4)
+    cp = s + 1 - 2 * lax.rem(s, 2)
+    far = 3 - s
+
+    def flat_peer(step):
+        peer = lax.rem(me + step, 16)
+        return {"seq": peer // 4, "fsdp": lax.rem(peer, 4)}
+
+    entry_barrier([flat_peer(step) for step in range(1, 16)])
+
+    def remote(src, dst, ss, rs, dev):
+        return pltpu.make_async_remote_copy(
+            src_ref=src, dst_ref=dst, send_sem=ss, recv_sem=rs, device_id=dev, device_id_type=MESH
+        )
+
+    def mod_copy(step):
+        return remote(
+            mod_ref, mod_all.at[me], mod_s.at[step - 1], mod_r.at[step - 1], flat_peer(step)
+        )
+
+    for step in range(1, 16):
+        mod_copy(step).start()
+
+    def lat_copy(side, k):
+        target = z + 1 if side == 0 else z - 1
+        shard = z - k if side == 0 else z + k
+        shard = jnp.clip(shard, 0, 3)
+        src = lat_ref if k == 0 else lat_all.at[shard]
+        return remote(
+            src, lat_all.at[shard], lat_s.at[side, k], lat_r.at[side, k], {"fsdp": target}
+        )
+
+    def sends(side, k):
+        return (z < 3) & (z - k >= 0) if side == 0 else (z > 0) & (z + k <= 3)
+
+    def gets(side, k):
+        return z - 1 - k >= 0 if side == 0 else z + 1 + k <= 3
+
+    def start_lat(k):
+        for side in range(2):
+            @pl.when(sends(side, k))
+            def _():
+                lat_copy(side, k).start()
+
+    def wait_lat(k):
+        for side in range(2):
+            @pl.when(gets(side, k))
+            def _():
+                remote(
+                    lat_ref,
+                    lat_all.at[jnp.clip(z - 1 - k if side == 0 else z + 1 + k, 0, 3)],
+                    lat_s.at[side, k], lat_r.at[side, k], {"fsdp": lax.rem(z + 1, 4)},
+                ).wait_recv()
+
+    start_lat(0)
+
+    def w_copy(kind, j):
+        if kind == 0:
+            return remote(w_ref.at[j], w_all.at[s, j], w_s.at[0, j], w_r.at[0, j], {"seq": yp})
+        if kind == 1:
+            return remote(w_ref.at[j], w_all.at[s, j], w_s.at[1, j], w_r.at[1, j], {"seq": cp})
+        return remote(w_all.at[yp, j], w_all.at[yp, j], w_s.at[2, j], w_r.at[2, j], {"seq": cp})
+
+    def w_wait(kind, j):
+        slot = (yp, cp, far)[kind]
+        remote(
+            w_ref.at[j], w_all.at[slot, j], w_s.at[kind, j], w_r.at[kind, j], {"seq": cp}
+        ).wait_recv()
+
+    order = (1, 2, 0)
+    for j in order:
+        w_copy(0, j).start()
+        w_copy(1, j).start()
+
+    local = [
+        pltpu.make_async_copy(w_ref, w_all.at[s], loc_sem.at[0]),
+        pltpu.make_async_copy(lat_ref, lat_all.at[z], loc_sem.at[1]),
+        pltpu.make_async_copy(ow_ref, ow_all.at[s], loc_sem.at[2]),
+        pltpu.make_async_copy(mod_ref, mod_all.at[me], loc_sem.at[3]),
+    ]
+    for copy in local:
+        copy.start()
+
+    @pl.when(s == 0)
+    def _():
+        kv_out[0] = jnp.zeros(kv_out.shape[1:], BF)
+
+    @pl.when(s == 3)
+    def _():
+        kv_out[2] = jnp.zeros(kv_out.shape[1:], BF)
+
+    for copy in local:
+        copy.wait()
+    for step in range(1, 16):
+        sender = lax.rem(me - step + 16, 16)
+        remote(
+            mod_ref, mod_all.at[sender], mod_s.at[step - 1], mod_r.at[step - 1], flat_peer(step)
+        ).wait_recv()
+    mod_out[...] = jnp.concatenate([mod_all[i] for i in range(16)], axis=1)
+
+    w_wait(0, order[0])
+    w_copy(2, order[0]).start()
+    wait_lat(0)
+    start_lat(1)
+    w_wait(0, order[1])
+    w_copy(2, order[1]).start()
+    wait_lat(1)
+    start_lat(2)
+    w_wait(0, order[2])
+    w_copy(2, order[2]).start()
+
+    ow_y = remote(ow_ref, ow_all.at[s], ow_s.at[0], ow_r.at[0], {"seq": yp})
+    ow_c = remote(ow_ref, ow_all.at[s], ow_s.at[1], ow_r.at[1], {"seq": cp})
+    ow_f = remote(ow_all.at[yp], ow_all.at[yp], ow_s.at[2], ow_r.at[2], {"seq": cp})
+    ow_y.start()
+    ow_c.start()
+    for j in order:
+        w_wait(1, j)
+        w_wait(2, j)
+
+    def kv_copy(side, i, zz):
+        src = kv_out.at[1, pl.ds(pl.multiple_of(zz * rows, rows), rows)]
+        dst = kv_out.at[0 if side == 0 else 2, pl.ds(pl.multiple_of(zz * rows, rows), rows)]
+        target = s + 1 if side == 0 else s - 1
+        return remote(src, dst, kv_s.at[side, i], kv_r.at[side, i], {"seq": target})
+
+    hi = z // 2
+
+    def shard_of(i):
+        return lax.rem(i + hi, 4)
+
+    width = w_ref.shape[1]
+    lane = 128
+
+    def one_shard(i, carry):
+        zz = shard_of(i)
+
+        @pl.when(i == 3)
+        def _():
+            wait_lat(2)
+
+        def norm_rows(r, c):
+            at = pl.ds(pl.multiple_of(r * 32, 32), 32)
+            values = lat_all[zz, at, :].astype(F32)
+            centre = jnp.mean(values, axis=-1, keepdims=True)
+            values = values - centre
+            spread = jnp.mean(values * values, axis=-1, keepdims=True)
+            normal = values * lax.rsqrt(spread + 1e-06)
+            nrm[at, :] = (normal * (1.0 + mod_out[1:2, :]) + mod_out[0:1, :]).astype(BF)
+            return c
+
+        lax.fori_loop(0, rows // 32, norm_rows, 0)
+        base = pl.ds(pl.multiple_of(zz * rows, rows), rows)
+        for j in order:
+            for col in range(0, width, 256):
+                acc = jnp.zeros((rows, 256), F32)
+                for t in range(4):
+                    acc = acc + jnp.dot(
+                        nrm[:, t * width : (t + 1) * width],
+                        w_all[t, j, :, col : col + 256],
+                        preferred_element_type=F32,
+                    )
+                for half in range(0, 256, lane):
+                    part = acc[:, half : half + lane]
+                    if j < 2:
+                        gain = (qg_ref if j == 0 else kg_ref)[...]
+                        scale = lax.rsqrt(jnp.mean(part * part, axis=-1, keepdims=True) + 1e-06)
+                        part = part * scale * gain
+                    part = part.astype(BF)
+                    first = col + half
+                    if j == 0:
+                        q_out[base, first : first + lane] = part
+                    else:
+                        first = first + (j - 1) * width
+                        kv_out[1, base, first : first + lane] = part
+            if j == 2:
+                @pl.when(s < 3)
+                def _():
+                    kv_copy(0, i, zz).start()
+
+                @pl.when(s > 0)
+                def _():
+                    kv_copy(1, i, zz).start()
+        return carry
+
+    lax.fori_loop(0, 4, one_shard, 0)
+
+    remote(ow_ref, ow_all.at[yp], ow_s.at[0], ow_r.at[0], {"seq": yp}).wait_recv()
+    ow_f.start()
+    remote(ow_ref, ow_all.at[cp], ow_s.at[1], ow_r.at[1], {"seq": cp}).wait_recv()
+    remote(ow_ref, ow_all.at[far], ow_s.at[2], ow_r.at[2], {"seq": cp}).wait_recv()
+    for i in range(4):
+        @pl.when(s > 0)
+        def _():
+            kv_copy(0, i, shard_of(i)).wait_recv()
+
+        @pl.when(s < 3)
+        def _():
+            kv_copy(1, i, shard_of(i)).wait_recv()
+    for i in range(4):
+        @pl.when(s < 3)
+        def _():
+            kv_copy(0, i, shard_of(i)).wait_send()
+
+        @pl.when(s > 0)
+        def _():
+            kv_copy(1, i, shard_of(i)).wait_send()
+    for step in range(1, 16):
+        mod_copy(step).wait_send()
+    for k in range(3):
+        for side in range(2):
+            @pl.when(sends(side, k))
+            def _():
+                lat_copy(side, k).wait_send()
+    for kind in range(3):
+        for j in range(3):
+            w_copy(kind, j).wait_send()
+    ow_y.wait_send()
+    ow_c.wait_send()
+    ow_f.wait_send()
+
+
+def gather_project(latents, w, ow, mod, q_gain, k_gain):
+    rows, model = latents.shape
+    width = w.shape[1]
+    vmem = pl.BlockSpec(memory_space=pltpu.VMEM)
+    dma = pltpu.SemaphoreType.DMA
+    return pl.pallas_call(
+        gather_kernel,
+        out_shape=(
+            jax.ShapeDtypeStruct((4 * rows, width), BF),
+            jax.ShapeDtypeStruct((3, 4 * rows, 2 * width), BF),
+            jax.ShapeDtypeStruct((4,) + ow.shape, BF),
+            jax.ShapeDtypeStruct((8, model), F32),
+        ),
+        in_specs=[vmem] * 6,
+        out_specs=(vmem,) * 4,
+        scratch_shapes=[
+            pltpu.VMEM((4, rows, model), BF),
+            pltpu.VMEM((4,) + w.shape, BF),
+            pltpu.VMEM((16,) + mod.shape, F32),
+            pltpu.VMEM((rows, model), BF),
+            dma((4,)), dma((15,)), dma((15,)), dma((2, 3)), dma((2, 3)),
+            dma((3, 3)), dma((3, 3)), dma((3,)), dma((3,)), dma((2, 4)), dma((2, 4)),
+        ],
+        compiler_params=pltpu.CompilerParams(
+            collective_id=0, has_side_effects=True, vmem_limit_bytes=VMEM_LIMIT
+        ),
+    )(latents, w, ow, mod, q_gain, k_gain)
+
+
+def attend_kernel(q_ref, k_ref, v_ref, bias_ref, o_ref):
+    span = q_ref.shape[0]
+    keys = k_ref.shape[0] * k_ref.shape[1]
+    scores = lax.dot_general(
+        q_ref[...], k_ref[...].reshape(keys, HD), (((1,), (1,)), ((), ())),
+        preferred_element_type=F32,
+    )
+    scores = (scores.reshape(span // TILE, TILE, keys) + bias_ref[...]).reshape(span, keys)
+    top = jnp.max(scores, axis=1, keepdims=True)
+    weights = jnp.exp2((scores - top) * (math.log2(math.e) / math.sqrt(HD)))
+    total = jnp.sum(weights, axis=1, keepdims=True)
+    mixed = jnp.dot(weights.astype(BF), v_ref[...].reshape(keys, HD), preferred_element_type=F32)
+    o_ref[...] = (mixed / total).astype(BF)
+
+
+def attend(q, kv, bias):
+    tokens, width = q.shape
+    heads = width // HD
+    span = 256
+    return pl.pallas_call(
+        attend_kernel,
+        grid=(heads, tokens // span),
+        out_shape=jax.ShapeDtypeStruct((tokens, width), BF),
+        in_specs=[
+            pl.BlockSpec((span, HD), lambda h, i: (i, h)),
+            pl.BlockSpec((3, tokens, HD), lambda h, i: (0, 0, h)),
+            pl.BlockSpec((3, tokens, HD), lambda h, i: (0, 0, heads + h)),
+            pl.BlockSpec((span // TILE, 1, 3 * tokens), lambda h, i: (i, 0, 0)),
+        ],
+        out_specs=pl.BlockSpec((span, HD), lambda h, i: (i, h)),
+        compiler_params=pltpu.CompilerParams(vmem_limit_bytes=VMEM_LIMIT),
+    )(q, kv, kv, bias)
+
+
+def out_kernel(att_ref, ow_ref, lat_ref, mod_ref, o_ref, sent, got, s_sem, r_sem):
+    z = lax.axis_index("fsdp")
+    rows = lat_ref.shape[0]
+    width = ow_ref.shape[1]
+    entry_barrier([{"fsdp": lax.rem(z + step, 4)} for step in range(1, 4)])
+
+    def copy(step):
+        return pltpu.make_async_remote_copy(
+            src_ref=sent.at[step], dst_ref=got.at[step],
+            send_sem=s_sem.at[step], recv_sem=r_sem.at[step],
+            device_id={"fsdp": lax.rem(z + step, 4)}, device_id_type=MESH,
+        )
+
+    for step in (2, 1, 3, 0):
+        goal = lax.rem(z + step, 4)
+        base = pl.ds(pl.multiple_of(goal * rows, rows), rows)
+        for t in range(4):
+            sent[step, :, t * width : (t + 1) * width] = jnp.dot(
+                att_ref[base, :], ow_ref[t], preferred_element_type=F32
+            ).astype(BF)
+        if step:
+            copy(step).start()
+    for step in range(1, 4):
+        copy(step).wait()
+
+    def finish(r, c):
+        at = pl.ds(pl.multiple_of(r * 32, 32), 32)
+        total = sent[0, at, :].astype(F32)
+        for step in range(1, 4):
+            total = total + got[step, at, :].astype(F32)
+        o_ref[at, :] = (lat_ref[at, :].astype(F32) + mod_ref[2:3, :] * total).astype(BF)
+        return c
+
+    lax.fori_loop(0, rows // 32, finish, 0)
+
+
+def out_project(att, ow_all, latents, mod_full):
+    vmem = pl.BlockSpec(memory_space=pltpu.VMEM)
+    rows, model = latents.shape
+    return pl.pallas_call(
+        out_kernel,
+        out_shape=jax.ShapeDtypeStruct(latents.shape, BF),
+        in_specs=[vmem] * 4,
+        out_specs=vmem,
+        scratch_shapes=[
+            pltpu.VMEM((4, rows, model), BF),
+            pltpu.VMEM((4, rows, model), BF),
+            pltpu.SemaphoreType.DMA((4,)),
+            pltpu.SemaphoreType.DMA((4,)),
+        ],
+        compiler_params=pltpu.CompilerParams(
+            collective_id=1, has_side_effects=True, vmem_limit_bytes=VMEM_LIMIT
+        ),
+    )(att, ow_all, latents, mod_full)
+
+
+def key_bias(tile_slot, win_start, block_idx):
+    blocks_total, spot_count = tile_slot.shape
+    ids_query = lax.dynamic_index_in_dim(tile_slot, block_idx, 0, keepdims=False)
+    window_row = lax.dynamic_index_in_dim(win_start, block_idx, 0, keepdims=False)
+    onehot = ids_query[:, None] == jnp.arange(spot_count, dtype=jnp.int32)[None, :]
+    corner = jnp.sum(jnp.where(onehot[:, :, None], window_row[None], 0), axis=1)
+    result = []
+    for offset in (-1, 0, 1):
+        key_time = block_idx + offset
+        ids_key = lax.dynamic_index_in_dim(
+            tile_slot, jnp.clip(key_time, 0, blocks_total - 1), 0, keepdims=False
+        )
+        row = (ids_key // GW)[None]
+        col = (ids_key % GW)[None]
+        inside = (corner[:, 0:1] <= key_time) & (key_time <= corner[:, 0:1] + 1)
+        inside = inside & (corner[:, 1:2] <= row) & (row <= corner[:, 1:2] + 2)
+        inside = inside & (corner[:, 2:3] <= col) & (col <= corner[:, 2:3] + 2)
+        result.append(inside)
+    inside = jnp.concatenate(result, axis=1)
+    bias = jnp.where(inside, 0.0, -1e30).astype(F32)
+    return jnp.repeat(bias, TILE, axis=1)[:, None, :]
+
+
+def fast_body(
+    latents, qkv_weight, out_weight, mod_weight, q_gain, k_gain, tile_slot, win_start, step_index
+):
+    signal = time_signal(step_index)
+    local_cols = mod_weight.shape[2]
+    own_mod = jnp.dot(
+        signal[None], mod_weight.reshape(FREQ, 3 * local_cols), preferred_element_type=F32
+    ).reshape(3, local_cols)
+    own_mod = jnp.pad(own_mod, ((0, 5), (0, 0)))
+    w = jnp.transpose(qkv_weight, (1, 0, 2))
+    bias = key_bias(tile_slot, win_start, lax.axis_index("seq"))
+    q, kv, ow_all, mod_full = gather_project(
+        latents, w, out_weight, own_mod, q_gain[None], k_gain[None]
+    )
+    att = attend(q, kv, bias)
+    return out_project(att, ow_all, latents, mod_full)
+
 
 def solution(mesh):
     in_specs = (
@@ -173,4 +580,8 @@
         P("group"),
     )
     out_specs = P(("group", "seq", "fsdp"), None)
-    return jax.shard_map(body, mesh=mesh, in_specs=in_specs, out_specs=out_specs, check_vma=False)
+    small = mesh.shape["seq"] == 4 and mesh.shape["fsdp"] == 4
+    return jax.shard_map(
+        fast_body if small else body,
+        mesh=mesh, in_specs=in_specs, out_specs=out_specs, check_vma=False,
+    )

time: 633 us -> 325 us (0.51); the launches traced: 623 us -> 324 us
  waiting for transfers between devices: 322 us -> 0 us
  Pallas kernels: 0 us -> 317 us
  matrix products: 135 us -> 0.18 us
  other arithmetic: 72.8 us -> 1.32 us
  local copies, waits for them, and re-layouts: 39 us -> 5.09 us
  blocking collectives: 31.8 us -> 0 us
  between operations: 15.2 us -> 0.78 us
  starting transfers between devices: 6.66 us -> 0 us
    pallas_call x0 -> x3, Pallas kernels: none -> 317 us  [the longest x1 153 us: gather_project(): pl.pallas_call(gather_kernel, out_shape=(jax.ShapeDtypeStruct((4 * rows,...]
    all_gather x3 -> x0, waiting for transfers between devices: 165 us -> none  [the longest x1 87.7 us: body(): qkv_full = lax.all_gather(qkv_weight, 'seq', axis=0, tiled=True)]
    dot_general x75 -> x1, matrix products: 135 us -> 0.18 us  [fast_body(): jnp.dot(signal[None], mod_weight.reshape(FREQ, 3 * local_cols), preferred...]
    reduce_scatter x1 -> x0, waiting for transfers between devices: 110 us -> none  [body(): lax.psum_scatter(jnp.dot(attended, out_full, preferred_element_type=jnp.f...]
    reduce_sum x10 -> x1, other arithmetic: 58.8 us -> 0.15 us  [key_bias(): corner = jnp.sum(jnp.where(onehot[:, :, None], window_row[None], 0), axis=1)]
    ppermute x2 -> x0, waiting for transfers between devices: 46.2 us -> none  [the longest x1 41.7 us: with_halo(): lax.ppermute(lax.slice_in_dim(block, block.shape[dim] - width, None, axis...]
    all_gather x1 -> x0, blocking collectives: 31.8 us -> none  [body(): modulation = lax.all_gather(own_mod, ('seq', 'fsdp'), axis=1, tiled=True)]
    slice x18 -> x0, local copies, waits for them, and re-layouts: 18.3 us -> none  [the longest x15 9.39 us: body(): allowed = visible[key_blk][lower:lower + query_span]]
  transfers between devices with their start and end apart: 6 -> 0, of which waited for: 5 -> 0; matrix products, arithmetic and copies ran while one was open for 32% -> 0% of each run, Pallas kernels for 0% -> 0%
where the time goes in v1:
time: 325 us; the launch traced here: 324 us
  Pallas kernels  317 us (98%)
  local copies, waits for them, and re-layouts  5.09 us (2%)
    pallas_call x1, Pallas kernels, gather_project(): pl.pallas_call(gather_kernel, out_shape=(jax.ShapeDtypeStruct((4 * rows,...  153 us
    pallas_call x1, Pallas kernels, out_project(): pl.pallas_call(out_kernel, out_shape=jax.ShapeDtypeStruct(latents.shape,...  124 us
    pallas_call x1, Pallas kernels, attend(): pl.pallas_call(attend_kernel, grid=(heads, tokens // span), out_shape=jax...  40.4 us

profile of v1, /device:TPU:9, one launch (start us, length us, event | category | flops | bytes accessed | tf_op | source)
XLA Modules:
  0.0 324.3 jit_solution(3081390110061527566)
XLA Ops:
  0.0 0.0 copy-start
  0.8 0.7 constant_dynamic-slice_fusion.3
  1.5 0.8 fusion.7
  2.4 0.1 iota_compare_fusion
  2.4 0.1 select_reduce_fusion
  2.6 0.1 compare_and_fusion.2
  2.7 0.1 add_select_fusion
  2.8 0.0 copy-done
  2.8 0.2 fusion
  3.0 0.6 pad.4.mod_ref
  3.6 0.2 broadcast_in_dim.58
  3.8 0.9 broadcast_in_dim_reshape.3.bias_ref
  4.7 152.6 %shard_map.91 = (bf16[1024,768]{1,0:T(8,128)(2,1)}, bf16[3,1024,1536]{2,1,0:T(8,128)(2,1)}, bf16[4,768,768]{2,1,0:T(8,128)(2,1)}, f32[8,3072]{1,0:T(8,128)}) custom-call(bf16[256,3072]{1,0:T(8,128)(2,1)} %lat_ref.3, bf16[3,768,768]{2,1,0:T(8,128)(2,1)} %bitcast.46, bf16[768,768]{1,0:T(8,128)(2,1)} %ow_ref.1, f32[8,192]{1,0:T(8,128)} %pad.4.mod_ref, ...), custom_call_target="tpu_custom_call" | custom-call | tf_op jit(solution)/shard_map/pallas_call | solution.py:415
  157.4 40.4 %shard_map.92.att_ref = bf16[1024,768]{1,0:T(8,128)(2,1)} custom-call(bf16[1024,768]{1,0:T(8,128)(2,1)} %get-tuple-element.9.q_ref, bf16[3,1024,1536]{2,1,0:T(8,128)(2,1)} %get-tuple-element.10.k_ref.v_ref, bf16[3,1024,1536]{2,1,0:T(8,128)(2,1)} %get-tuple-element.10.k_ref.v_ref, f32[16,1,3072]{2,1,0:T(1,128)} %broadcast_in_dim_reshape.3.bias_ref), custom_call_target="tpu_custom_call" | custom-call | tf_op jit(solution)/shard_map/pallas_call | solution.py:458
  197.8 123.9 %shard_map.93 = bf16[256,3072]{1,0:T(8,128)(2,1)} custom-call(bf16[1024,768]{1,0:T(8,128)(2,1)} %shard_map.92.att_ref, bf16[4,768,768]{2,1,0:T(8,128)(2,1)} %get-tuple-element.11.ow_ref, bf16[256,3072]{1,0:T(8,128)(2,1)} %lat_ref.3, f32[8,3072]{1,0:T(8,128)} %get-tuple-element.12.mod_ref), custom_call_target="tpu_custom_call" | custom-call | tf_op jit(solution)/shard_map/pallas_call | solution.py:512
  321.6 2.7 copy.20
  (9 shorter events, 0.1 us)
Async XLA Ops:
  0.0 2.8 copy-start

commit v2 on v1

--- a/solution.py
+++ b/solution.py
@@ -188,12 +188,17 @@
     yp = lax.rem(s + 2, 4)
     cp = s + 1 - 2 * lax.rem(s, 2)
     far = 3 - s
+    g = lax.axis_index("group")
+    across = {"group": 1 - g}
+    half = w_ref.shape[1] // 2
+    mine = pl.ds(pl.multiple_of(g * half, half), half)
+    theirs = pl.ds(pl.multiple_of((1 - g) * half, half), half)
 
     def flat_peer(step):
         peer = lax.rem(me + step, 16)
         return {"seq": peer // 4, "fsdp": lax.rem(peer, 4)}
 
-    entry_barrier([flat_peer(step) for step in range(1, 16)])
+    entry_barrier([flat_peer(step) for step in range(1, 16)] + [across])
 
     def remote(src, dst, ss, rs, dev):
         return pltpu.make_async_remote_copy(
@@ -241,18 +246,45 @@
 
     start_lat(0)
 
+    def spread(own, full, sems_s, sems_r):
+        def copy(kind):
+            src, dst, dev = (
+                (own.at[mine], full.at[s, mine], {"seq": yp}),
+                (own, full.at[s], {"seq": cp}),
+                (full.at[yp, mine], full.at[yp, mine], {"seq": cp}),
+                (full.at[yp, mine], full.at[yp, mine], across),
+                (full.at[yp, theirs], full.at[yp, theirs], {"seq": cp}),
+            )[kind]
+            return remote(src, dst, sems_s.at[kind], sems_r.at[kind], dev)
+
+        def wait(kind):
+            slot = (yp, cp, far, yp, far)[kind]
+            part = (mine, None, mine, theirs, theirs)[kind]
+            src = own if part is None else own.at[part]
+            dst = full.at[slot] if part is None else full.at[slot, part]
+            remote(src, dst, sems_s.at[kind], sems_r.at[kind], {"seq": cp}).wait_recv()
+
+        return copy, wait
+
+    w_moves = [
+        spread(w_ref.at[j], w_all.at[j], w_s.at[j], w_r.at[j]) for j in range(3)
+    ]
+    ow_copy, ow_wait = spread(ow_ref, ow_all, ow_s, ow_r)
+
     def w_copy(kind, j):
-        if kind == 0:
-            return remote(w_ref.at[j], w_all.at[s, j], w_s.at[0, j], w_r.at[0, j], {"seq": yp})
-        if kind == 1:
-            return remote(w_ref.at[j], w_all.at[s, j], w_s.at[1, j], w_r.at[1, j], {"seq": cp})
-        return remote(w_all.at[yp, j], w_all.at[yp, j], w_s.at[2, j], w_r.at[2, j], {"seq": cp})
+        return w_moves[j][0](kind)
 
     def w_wait(kind, j):
-        slot = (yp, cp, far)[kind]
-        remote(
-            w_ref.at[j], w_all.at[slot, j], w_s.at[kind, j], w_r.at[kind, j], {"seq": cp}
-        ).wait_recv()
+        w_moves[j][1](kind)
+
+    def after_y(copy, wait):
+        wait(0)
+        copy(2).start()
+        copy(3).start()
+
+    def after_x(copy, wait):
+        wait(3)
+        copy(4).start()
 
     order = (1, 2, 0)
     for j in order:
@@ -260,7 +292,9 @@
         w_copy(1, j).start()
 
     local = [
-        pltpu.make_async_copy(w_ref, w_all.at[s], loc_sem.at[0]),
+        pltpu.make_async_copy(w_ref.at[0], w_all.at[0, s], loc_sem.at[0]),
+        pltpu.make_async_copy(w_ref.at[1], w_all.at[1, s], loc_sem.at[4]),
+        pltpu.make_async_copy(w_ref.at[2], w_all.at[2, s], loc_sem.at[5]),
         pltpu.make_async_copy(lat_ref, lat_all.at[z], loc_sem.at[1]),
         pltpu.make_async_copy(ow_ref, ow_all.at[s], loc_sem.at[2]),
         pltpu.make_async_copy(mod_ref, mod_all.at[me], loc_sem.at[3]),
@@ -285,25 +319,19 @@
         ).wait_recv()
     mod_out[...] = jnp.concatenate([mod_all[i] for i in range(16)], axis=1)
 
-    w_wait(0, order[0])
-    w_copy(2, order[0]).start()
+    after_y(*w_moves[order[0]])
+    after_y(*w_moves[order[1]])
+    after_x(*w_moves[order[0]])
     wait_lat(0)
     start_lat(1)
-    w_wait(0, order[1])
-    w_copy(2, order[1]).start()
-    wait_lat(1)
-    start_lat(2)
-    w_wait(0, order[2])
-    w_copy(2, order[2]).start()
-
-    ow_y = remote(ow_ref, ow_all.at[s], ow_s.at[0], ow_r.at[0], {"seq": yp})
-    ow_c = remote(ow_ref, ow_all.at[s], ow_s.at[1], ow_r.at[1], {"seq": cp})
-    ow_f = remote(ow_all.at[yp], ow_all.at[yp], ow_s.at[2], ow_r.at[2], {"seq": cp})
-    ow_y.start()
-    ow_c.start()
+    after_y(*w_moves[order[2]])
+    ow_copy(0).start()
+    ow_copy(1).start()
+    after_x(*w_moves[order[1]])
+    after_x(*w_moves[order[2]])
     for j in order:
-        w_wait(1, j)
-        w_wait(2, j)
+        for kind in (1, 2, 4):
+            w_wait(kind, j)
 
     def kv_copy(side, i, zz):
         src = kv_out.at[1, pl.ds(pl.multiple_of(zz * rows, rows), rows)]
@@ -314,13 +342,23 @@
     hi = z // 2
 
     def shard_of(i):
-        return lax.rem(i + hi, 4)
+        return i + hi * (3 - 2 * i)
 
     width = w_ref.shape[1]
     lane = 128
 
     def one_shard(i, carry):
         zz = shard_of(i)
+
+        @pl.when(i == 1)
+        def _():
+            after_y(ow_copy, ow_wait)
+
+        @pl.when(i == 2)
+        def _():
+            wait_lat(1)
+            start_lat(2)
+            after_x(ow_copy, ow_wait)
 
         @pl.when(i == 3)
         def _():
@@ -344,7 +382,7 @@
                 for t in range(4):
                     acc = acc + jnp.dot(
                         nrm[:, t * width : (t + 1) * width],
-                        w_all[t, j, :, col : col + 256],
+                        w_all[j, t, :, col : col + 256],
                         preferred_element_type=F32,
                     )
                 for half in range(0, 256, lane):
@@ -372,10 +410,8 @@
 
     lax.fori_loop(0, 4, one_shard, 0)
 
-    remote(ow_ref, ow_all.at[yp], ow_s.at[0], ow_r.at[0], {"seq": yp}).wait_recv()
-    ow_f.start()
-    remote(ow_ref, ow_all.at[cp], ow_s.at[1], ow_r.at[1], {"seq": cp}).wait_recv()
-    remote(ow_ref, ow_all.at[far], ow_s.at[2], ow_r.at[2], {"seq": cp}).wait_recv()
+    for kind in (1, 2, 4):
+        ow_wait(kind)
     for i in range(4):
         @pl.when(s > 0)
         def _():
@@ -399,12 +435,10 @@
             @pl.when(sends(side, k))
             def _():
                 lat_copy(side, k).wait_send()
-    for kind in range(3):
+    for kind in range(5):
         for j in range(3):
             w_copy(kind, j).wait_send()
-    ow_y.wait_send()
-    ow_c.wait_send()
-    ow_f.wait_send()
+        ow_copy(kind).wait_send()
 
 
 def gather_project(latents, w, ow, mod, q_gain, k_gain):
@@ -424,11 +458,11 @@
         out_specs=(vmem,) * 4,
         scratch_shapes=[
             pltpu.VMEM((4, rows, model), BF),
-            pltpu.VMEM((4,) + w.shape, BF),
+            pltpu.VMEM((3, 4) + w.shape[1:], BF),
             pltpu.VMEM((16,) + mod.shape, F32),
             pltpu.VMEM((rows, model), BF),
-            dma((4,)), dma((15,)), dma((15,)), dma((2, 3)), dma((2, 3)),
-            dma((3, 3)), dma((3, 3)), dma((3,)), dma((3,)), dma((2, 4)), dma((2, 4)),
+            dma((6,)), dma((15,)), dma((15,)), dma((2, 3)), dma((2, 3)),
+            dma((3, 5)), dma((3, 5)), dma((5,)), dma((5,)), dma((2, 4)), dma((2, 4)),
         ],
         compiler_params=pltpu.CompilerParams(
             collective_id=0, has_side_effects=True, vmem_limit_bytes=VMEM_LIMIT
@@ -436,85 +470,122 @@
     )(latents, w, ow, mod, q_gain, k_gain)
 
 
-def attend_kernel(q_ref, k_ref, v_ref, bias_ref, o_ref):
-    span = q_ref.shape[0]
-    keys = k_ref.shape[0] * k_ref.shape[1]
-    scores = lax.dot_general(
-        q_ref[...], k_ref[...].reshape(keys, HD), (((1,), (1,)), ((), ())),
-        preferred_element_type=F32,
-    )
-    scores = (scores.reshape(span // TILE, TILE, keys) + bias_ref[...]).reshape(span, keys)
-    top = jnp.max(scores, axis=1, keepdims=True)
-    weights = jnp.exp2((scores - top) * (math.log2(math.e) / math.sqrt(HD)))
-    total = jnp.sum(weights, axis=1, keepdims=True)
-    mixed = jnp.dot(weights.astype(BF), v_ref[...].reshape(keys, HD), preferred_element_type=F32)
-    o_ref[...] = (mixed / total).astype(BF)
-
-
-def attend(q, kv, bias):
-    tokens, width = q.shape
-    heads = width // HD
-    span = 256
-    return pl.pallas_call(
-        attend_kernel,
-        grid=(heads, tokens // span),
-        out_shape=jax.ShapeDtypeStruct((tokens, width), BF),
-        in_specs=[
-            pl.BlockSpec((span, HD), lambda h, i: (i, h)),
-            pl.BlockSpec((3, tokens, HD), lambda h, i: (0, 0, h)),
-            pl.BlockSpec((3, tokens, HD), lambda h, i: (0, 0, heads + h)),
-            pl.BlockSpec((span // TILE, 1, 3 * tokens), lambda h, i: (i, 0, 0)),
-        ],
-        out_specs=pl.BlockSpec((span, HD), lambda h, i: (i, h)),
-        compiler_params=pltpu.CompilerParams(vmem_limit_bytes=VMEM_LIMIT),
-    )(q, kv, kv, bias)
-
-
-def out_kernel(att_ref, ow_ref, lat_ref, mod_ref, o_ref, sent, got, s_sem, r_sem):
+def attend_out_kernel(
+    q_ref, kv_ref, bias_ref, ow_ref, lat_ref, mod_ref, o_ref, att, sent, got, s_sem, r_sem
+):
     z = lax.axis_index("fsdp")
     rows = lat_ref.shape[0]
     width = ow_ref.shape[1]
+    heads = width // HD
+    keys = kv_ref.shape[0] * kv_ref.shape[1]
+    hi = z // 2
+    far_outer = 3 - 3 * hi
+    far_inner = 2 - hi
+    near = z + 1 - 2 * lax.rem(z, 2)
+    inner = (z == 1) | (z == 2)
     entry_barrier([{"fsdp": lax.rem(z + step, 4)} for step in range(1, 4)])
 
-    def copy(step):
+    def copy(src, dst, goal):
         return pltpu.make_async_remote_copy(
-            src_ref=sent.at[step], dst_ref=got.at[step],
-            send_sem=s_sem.at[step], recv_sem=r_sem.at[step],
-            device_id={"fsdp": lax.rem(z + step, 4)}, device_id_type=MESH,
-        )
-
-    for step in (2, 1, 3, 0):
-        goal = lax.rem(z + step, 4)
+            src_ref=sent.at[src], dst_ref=got.at[dst],
+            send_sem=s_sem.at[src], recv_sem=r_sem.at[dst],
+            device_id={"fsdp": goal}, device_id_type=MESH,
+        )
+
+    to_near = [copy(src, src, near) for src in range(3)]
+    to_far = [copy(0, 3, far_outer), copy(1, 3, far_inner)]
+
+    def block(slot, goal):
         base = pl.ds(pl.multiple_of(goal * rows, rows), rows)
+        tiles = rows // TILE
+
+        def head(h, c):
+            at = pl.ds(pl.multiple_of(h * HD, HD), HD)
+            values_at = pl.ds(pl.multiple_of((heads + h) * HD, HD), HD)
+            scores = lax.dot_general(
+                q_ref[base, at], kv_ref[:, :, at].reshape(keys, HD), (((1,), (1,)), ((), ())),
+                preferred_element_type=F32,
+            )
+            bias = bias_ref[pl.ds(goal * tiles, tiles)]
+            scores = (scores.reshape(tiles, TILE, keys) + bias).reshape(rows, keys)
+            top = jnp.max(scores, axis=1, keepdims=True)
+            weights = jnp.exp2((scores - top) * (math.log2(math.e) / math.sqrt(HD)))
+            total = jnp.sum(weights, axis=1, keepdims=True)
+            mixed = jnp.dot(
+                weights.astype(BF), kv_ref[:, :, values_at].reshape(keys, HD),
+                preferred_element_type=F32,
+            )
+            att[:, at] = (mixed / total).astype(BF)
+            return c
+
+        lax.fori_loop(0, heads, head, 0)
         for t in range(4):
-            sent[step, :, t * width : (t + 1) * width] = jnp.dot(
-                att_ref[base, :], ow_ref[t], preferred_element_type=F32
+            sent[slot, :, t * width : (t + 1) * width] = jnp.dot(
+                att[...], ow_ref[t], preferred_element_type=F32
             ).astype(BF)
-        if step:
-            copy(step).start()
-    for step in range(1, 4):
-        copy(step).wait()
+
+    def add_near(slot):
+        to_near[slot].wait_recv()
+
+        def add(r, c):
+            at = pl.ds(pl.multiple_of(r * 32, 32), 32)
+            sent[slot, at, :] = (
+                sent[slot, at, :].astype(F32) + got[slot, at, :].astype(F32)
+            ).astype(BF)
+            return c
+
+        lax.fori_loop(0, rows // 32, add, 0)
+        to_far[slot].start()
+
+    def step(i, c):
+        goal = jnp.where(i == 0, far_outer, jnp.where(i == 1, far_inner, jnp.where(i == 2, near, z)))
+        block(i, goal)
+        for slot in range(2):
+            @pl.when(jnp.logical_not(inner) & (i == slot))
+            def _():
+                to_near[slot].start()
+
+        @pl.when(i == 2)
+        def _():
+            to_near[2].start()
+
+        @pl.when(inner & (i == 2))
+        def _():
+            add_near(0)
+
+        @pl.when(inner & (i == 3))
+        def _():
+            add_near(1)
+
+        return c
+
+    lax.fori_loop(0, 4, step, 0)
+    to_near[2].wait_recv()
+    copy(0, 3, far_outer).wait_recv()
+    for slot in range(3):
+        to_near[slot].wait_send()
 
     def finish(r, c):
         at = pl.ds(pl.multiple_of(r * 32, 32), 32)
-        total = sent[0, at, :].astype(F32)
-        for step in range(1, 4):
-            total = total + got[step, at, :].astype(F32)
+        total = sent[3, at, :].astype(F32)
+        total = total + got[2, at, :].astype(F32)
+        total = total + got[3, at, :].astype(F32)
         o_ref[at, :] = (lat_ref[at, :].astype(F32) + mod_ref[2:3, :] * total).astype(BF)
         return c
 
     lax.fori_loop(0, rows // 32, finish, 0)
 
 
-def out_project(att, ow_all, latents, mod_full):
+def attend_out(q, kv, bias, ow_all, latents, mod_full):
     vmem = pl.BlockSpec(memory_space=pltpu.VMEM)
     rows, model = latents.shape
     return pl.pallas_call(
-        out_kernel,
+        attend_out_kernel,
         out_shape=jax.ShapeDtypeStruct(latents.shape, BF),
-        in_specs=[vmem] * 4,
+        in_specs=[vmem] * 6,
         out_specs=vmem,
         scratch_shapes=[
+            pltpu.VMEM((rows, q.shape[1]), BF),
             pltpu.VMEM((4, rows, model), BF),
             pltpu.VMEM((4, rows, model), BF),
             pltpu.SemaphoreType.DMA((4,)),
@@ -523,7 +594,7 @@
         compiler_params=pltpu.CompilerParams(
             collective_id=1, has_side_effects=True, vmem_limit_bytes=VMEM_LIMIT
         ),
-    )(att, ow_all, latents, mod_full)
+    )(q, kv, bias, ow_all, latents, mod_full)
 
 
 def key_bias(tile_slot, win_start, block_idx):
@@ -563,8 +634,7 @@
     q, kv, ow_all, mod_full = gather_project(
         latents, w, out_weight, own_mod, q_gain[None], k_gain[None]
     )
-    att = attend(q, kv, bias)
-    return out_project(att, ow_all, latents, mod_full)
+    return attend_out(q, kv, bias, ow_all, latents, mod_full)
 
 
 def solution(mesh):

time: 325 us -> 261 us (0.80)
  Pallas kernels: 317 us -> 253 us
    pallas_call x1, Pallas kernels: 153 us -> 118 us  [gather_project(): pl.pallas_call(gather_kernel, out_shape=(jax.ShapeDtypeStruct((4 * rows,...]
    pallas_call x2 -> x1, Pallas kernels: 164 us -> 135 us  [attend_out(): pl.pallas_call(attend_out_kernel, out_shape=jax.ShapeDtypeStruct(latents....]
where the time goes in v2:
time: 261 us; the launch traced here: 260 us
  Pallas kernels  253 us (97%)
  local copies, waits for them, and re-layouts  5.09 us (2%)
    pallas_call x1, Pallas kernels, attend_out(): pl.pallas_call(attend_out_kernel, out_shape=jax.ShapeDtypeStruct(latents....  135 us
    pallas_call x1, Pallas kernels, gather_project(): pl.pallas_call(gather_kernel, out_shape=(jax.ShapeDtypeStruct((4 * rows,...  118 us

profile of v2, /device:TPU:9, one launch (start us, length us, event | category | flops | bytes accessed | tf_op | source)
XLA Modules:
  0.0 260.3 jit_solution(12398745777110760084)
XLA Ops:
  0.0 0.0 copy-start
  0.8 0.7 constant_dynamic-slice_fusion.3
  1.5 0.8 fusion.7
  2.4 0.1 iota_compare_fusion
  2.4 0.1 select_reduce_fusion
  2.6 0.1 compare_and_fusion.2
  2.7 0.1 add_select_fusion
  2.8 0.0 copy-done
  2.8 0.2 fusion
  3.0 0.6 pad.4.mod_ref
  3.6 0.2 broadcast_in_dim.58
  3.8 0.9 broadcast_in_dim_reshape.3.bias_ref
  4.7 118.3 %shard_map.91 = (bf16[1024,768]{1,0:T(8,128)(2,1)}, bf16[3,1024,1536]{2,1,0:T(8,128)(2,1)}, bf16[4,768,768]{2,1,0:T(8,128)(2,1)}, f32[8,3072]{1,0:T(8,128)}) custom-call(bf16[256,3072]{1,0:T(8,128)(2,1)} %lat_ref.3, bf16[3,768,768]{2,1,0:T(8,128)(2,1)} %bitcast.46, bf16[768,768]{1,0:T(8,128)(2,1)} %ow_ref.1, f32[8,192]{1,0:T(8,128)} %pad.4.mod_ref, ...), custom_call_target="tpu_custom_call" | custom-call | tf_op jit(solution)/shard_map/pallas_call | solution.py:449
  123.1 134.6 %shard_map.92 = bf16[256,3072]{1,0:T(8,128)(2,1)} custom-call(bf16[1024,768]{1,0:T(8,128)(2,1)} %get-tuple-element.9.q_ref, bf16[3,1024,1536]{2,1,0:T(8,128)(2,1)} %get-tuple-element.10.kv_ref, f32[16,1,3072]{2,1,0:T(1,128)} %broadcast_in_dim_reshape.3.bias_ref, bf16[4,768,768]{2,1,0:T(8,128)(2,1)} %get-tuple-element.11.ow_ref, bf16[256,3072]{1,0:T(8,128)(2,1)} %lat_ref.3, ...), custom_call_target="tpu_custom_call" | custom-call | tf_op jit(solution)/shard_map/pallas_call | solution.py:582
  257.7 2.7 %copy.20 = bf16[256,3072]{1,0:T(8,128)(2,1)} copy(bf16[256,3072]{1,0:T(8,128)(2,1)} %shard_map.92) | data formatting | bytes 3145728
  (9 shorter events, 0.1 us)
Async XLA Ops:
  0.0 2.8 %copy-start = (bf16[256,3,192]{0,2,1:T(8,128)(2,1)S(1)}, bf16[256,3,192]{0,2,1:T(8,128)(2,1)}, u32[]{:S(2)}) copy-start(bf16[256,3,192]{0,2,1:T(8,128)(2,1)} %param.12) | copy-start | bytes 884740

commit v3 on v2

--- a/solution.py
+++ b/solution.py
@@ -329,6 +329,8 @@
     ow_copy(1).start()
     after_x(*w_moves[order[1]])
     after_x(*w_moves[order[2]])
+    wait_lat(1)
+    start_lat(2)
     for j in order:
         for kind in (1, 2, 4):
             w_wait(kind, j)
@@ -356,8 +358,6 @@
 
         @pl.when(i == 2)
         def _():
-            wait_lat(1)
-            start_lat(2)
             after_x(ow_copy, ow_wait)
 
         @pl.when(i == 3)

time: 261 us -> 261 us (level)
    pallas_call x1, Pallas kernels: 118 us -> 132 us  [gather_project(): pl.pallas_call(gather_kernel, out_shape=(jax.ShapeDtypeStruct((4 * rows,...]
    pallas_call x1, Pallas kernels: 135 us -> 121 us  [attend_out(): pl.pallas_call(attend_out_kernel, out_shape=jax.ShapeDtypeStruct(latents....]
where the time goes in v3:
time: 261 us; the launch traced here: 260 us
  Pallas kernels  253 us (97%)
  local copies, waits for them, and re-layouts  5.09 us (2%)
    pallas_call x1, Pallas kernels, gather_project(): pl.pallas_call(gather_kernel, out_shape=(jax.ShapeDtypeStruct((4 * rows,...  132 us
    pallas_call x1, Pallas kernels, attend_out(): pl.pallas_call(attend_out_kernel, out_shape=jax.ShapeDtypeStruct(latents....  121 us

profile of v3, /device:TPU:9, one launch (start us, length us, event | category | flops | bytes accessed | tf_op | source)
XLA Modules:
  0.0 260.3 jit_solution(12521595182102490542)
XLA Ops:
  0.0 0.0 copy-start
  0.8 0.7 constant_dynamic-slice_fusion.3
  1.5 0.8 fusion.7
  2.4 0.1 iota_compare_fusion
  2.4 0.1 select_reduce_fusion
  2.6 0.1 compare_and_fusion.2
  2.7 0.1 add_select_fusion
  2.8 0.0 copy-done
  2.8 0.2 fusion
  3.0 0.6 pad.4.mod_ref
  3.6 0.2 broadcast_in_dim.58
  3.8 0.9 broadcast_in_dim_reshape.3.bias_ref
  4.7 131.8 %shard_map.91 = (bf16[1024,768]{1,0:T(8,128)(2,1)}, bf16[3,1024,1536]{2,1,0:T(8,128)(2,1)}, bf16[4,768,768]{2,1,0:T(8,128)(2,1)}, f32[8,3072]{1,0:T(8,128)}) custom-call(bf16[256,3072]{1,0:T(8,128)(2,1)} %lat_ref.3, bf16[3,768,768]{2,1,0:T(8,128)(2,1)} %bitcast.46, bf16[768,768]{1,0:T(8,128)(2,1)} %ow_ref.1, f32[8,192]{1,0:T(8,128)} %pad.4.mod_ref, ...), custom_call_target="tpu_custom_call" | custom-call | tf_op jit(solution)/shard_map/pallas_call | solution.py:449
  136.5 121.2 %shard_map.92 = bf16[256,3072]{1,0:T(8,128)(2,1)} custom-call(bf16[1024,768]{1,0:T(8,128)(2,1)} %get-tuple-element.9.q_ref, bf16[3,1024,1536]{2,1,0:T(8,128)(2,1)} %get-tuple-element.10.kv_ref, f32[16,1,3072]{2,1,0:T(1,128)} %broadcast_in_dim_reshape.3.bias_ref, bf16[4,768,768]{2,1,0:T(8,128)(2,1)} %get-tuple-element.11.ow_ref, bf16[256,3072]{1,0:T(8,128)(2,1)} %lat_ref.3, ...), custom_call_target="tpu_custom_call" | custom-call | tf_op jit(solution)/shard_map/pallas_call | solution.py:582
  257.7 2.7 %copy.20 = bf16[256,3072]{1,0:T(8,128)(2,1)} copy(bf16[256,3072]{1,0:T(8,128)(2,1)} %shard_map.92) | data formatting | bytes 3145728
  (9 shorter events, 0.1 us)
Async XLA Ops:
  0.0 2.8 %copy-start = (bf16[256,3,192]{0,2,1:T(8,128)(2,1)S(1)}, bf16[256,3,192]{0,2,1:T(8,128)(2,1)}, u32[]{:S(2)}) copy-start(bf16[256,3,192]{0,2,1:T(8,128)(2,1)} %param.12) | copy-start | bytes 884740

commit v4 on v3

--- a/solution.py
+++ b/solution.py
@@ -175,11 +175,12 @@
     pl.semaphore_wait(barrier, len(peers))
 
 
-def gather_kernel(
-    lat_ref, w_ref, ow_ref, mod_ref, qg_ref, kg_ref,
+def block_kernel(
+    lat_ref, w_ref, ow_ref, mod_ref, qg_ref, kg_ref, bias_ref,
+    o_ref,
     q_out, kv_out, ow_all, mod_out,
-    lat_all, w_all, mod_all, nrm,
-    loc_sem, mod_s, mod_r, lat_s, lat_r, w_s, w_r, ow_s, ow_r, kv_s, kv_r,
+    lat_all, w_all, mod_all, nrm, att,
+    loc_sem, mod_s, mod_r, lat_s, lat_r, w_s, w_r, ow_s, ow_r, kv_s, kv_r, s_sem, r_sem, ready,
 ):
     s = lax.axis_index("seq")
     z = lax.axis_index("fsdp")
@@ -410,26 +411,6 @@
 
     lax.fori_loop(0, 4, one_shard, 0)
 
-    for kind in (1, 2, 4):
-        ow_wait(kind)
-    for i in range(4):
-        @pl.when(s > 0)
-        def _():
-            kv_copy(0, i, shard_of(i)).wait_recv()
-
-        @pl.when(s < 3)
-        def _():
-            kv_copy(1, i, shard_of(i)).wait_recv()
-    for i in range(4):
-        @pl.when(s < 3)
-        def _():
-            kv_copy(0, i, shard_of(i)).wait_send()
-
-        @pl.when(s > 0)
-        def _():
-            kv_copy(1, i, shard_of(i)).wait_send()
-    for step in range(1, 16):
-        mod_copy(step).wait_send()
     for k in range(3):
         for side in range(2):
             @pl.when(sends(side, k))
@@ -438,64 +419,39 @@
     for kind in range(5):
         for j in range(3):
             w_copy(kind, j).wait_send()
-        ow_copy(kind).wait_send()
-
-
-def gather_project(latents, w, ow, mod, q_gain, k_gain):
-    rows, model = latents.shape
-    width = w.shape[1]
-    vmem = pl.BlockSpec(memory_space=pltpu.VMEM)
-    dma = pltpu.SemaphoreType.DMA
-    return pl.pallas_call(
-        gather_kernel,
-        out_shape=(
-            jax.ShapeDtypeStruct((4 * rows, width), BF),
-            jax.ShapeDtypeStruct((3, 4 * rows, 2 * width), BF),
-            jax.ShapeDtypeStruct((4,) + ow.shape, BF),
-            jax.ShapeDtypeStruct((8, model), F32),
-        ),
-        in_specs=[vmem] * 6,
-        out_specs=(vmem,) * 4,
-        scratch_shapes=[
-            pltpu.VMEM((4, rows, model), BF),
-            pltpu.VMEM((3, 4) + w.shape[1:], BF),
-            pltpu.VMEM((16,) + mod.shape, F32),
-            pltpu.VMEM((rows, model), BF),
-            dma((6,)), dma((15,)), dma((15,)), dma((2, 3)), dma((2, 3)),
-            dma((3, 5)), dma((3, 5)), dma((5,)), dma((5,)), dma((2, 4)), dma((2, 4)),
-        ],
-        compiler_params=pltpu.CompilerParams(
-            collective_id=0, has_side_effects=True, vmem_limit_bytes=VMEM_LIMIT
-        ),
-    )(latents, w, ow, mod, q_gain, k_gain)
-
-
-def attend_out_kernel(
-    q_ref, kv_ref, bias_ref, ow_ref, lat_ref, mod_ref, o_ref, att, sent, got, s_sem, r_sem
-):
-    z = lax.axis_index("fsdp")
-    rows = lat_ref.shape[0]
-    width = ow_ref.shape[1]
+    for step in range(1, 4):
+        pl.semaphore_signal(
+            ready, inc=1, device_id={"fsdp": lax.rem(z + step, 4)}, device_id_type=MESH
+        )
+    for i in range(4):
+        @pl.when(s > 0)
+        def _():
+            kv_copy(0, i, shard_of(i)).wait_recv()
+
+        @pl.when(s < 3)
+        def _():
+            kv_copy(1, i, shard_of(i)).wait_recv()
+
     heads = width // HD
-    keys = kv_ref.shape[0] * kv_ref.shape[1]
-    hi = z // 2
+    keys = 3 * 4 * rows
     far_outer = 3 - 3 * hi
     far_inner = 2 - hi
     near = z + 1 - 2 * lax.rem(z, 2)
     inner = (z == 1) | (z == 2)
-    entry_barrier([{"fsdp": lax.rem(z + step, 4)} for step in range(1, 4)])
-
-    def copy(src, dst, goal):
-        return pltpu.make_async_remote_copy(
-            src_ref=sent.at[src], dst_ref=got.at[dst],
-            send_sem=s_sem.at[src], recv_sem=r_sem.at[dst],
-            device_id={"fsdp": goal}, device_id_type=MESH,
-        )
-
-    to_near = [copy(src, src, near) for src in range(3)]
-    to_far = [copy(0, 3, far_outer), copy(1, 3, far_inner)]
-
-    def block(slot, goal):
+
+    def slab(n):
+        if isinstance(n, int):
+            return w_all.at[n // 3, :, n % 3 * rows : (n % 3 + 1) * rows, :]
+        at = pl.ds(pl.multiple_of(lax.rem(n, 3) * rows, rows), rows)
+        return w_all.at[n // 3, :, at, :]
+
+    def send(src, dst, goal):
+        return remote(slab(src), slab(4 + dst), s_sem.at[src], r_sem.at[dst], {"fsdp": goal})
+
+    to_near = [send(src, src, near) for src in range(3)]
+    to_far = [send(0, 3, far_outer), send(1, 3, far_inner)]
+
+    def attend_rows(goal):
         base = pl.ds(pl.multiple_of(goal * rows, rows), rows)
         tiles = rows // TILE
 
@@ -503,7 +459,7 @@
             at = pl.ds(pl.multiple_of(h * HD, HD), HD)
             values_at = pl.ds(pl.multiple_of((heads + h) * HD, HD), HD)
             scores = lax.dot_general(
-                q_ref[base, at], kv_ref[:, :, at].reshape(keys, HD), (((1,), (1,)), ((), ())),
+                q_out[base, at], kv_out[:, :, at].reshape(keys, HD), (((1,), (1,)), ((), ())),
                 preferred_element_type=F32,
             )
             bias = bias_ref[pl.ds(goal * tiles, tiles)]
@@ -512,26 +468,21 @@
             weights = jnp.exp2((scores - top) * (math.log2(math.e) / math.sqrt(HD)))
             total = jnp.sum(weights, axis=1, keepdims=True)
             mixed = jnp.dot(
-                weights.astype(BF), kv_ref[:, :, values_at].reshape(keys, HD),
+                weights.astype(BF), kv_out[:, :, values_at].reshape(keys, HD),
                 preferred_element_type=F32,
             )
             att[:, at] = (mixed / total).astype(BF)
             return c
 
         lax.fori_loop(0, heads, head, 0)
-        for t in range(4):
-            sent[slot, :, t * width : (t + 1) * width] = jnp.dot(
-                att[...], ow_ref[t], preferred_element_type=F32
-            ).astype(BF)
 
     def add_near(slot):
         to_near[slot].wait_recv()
+        dst, src = slab(slot), slab(4 + slot)
 
         def add(r, c):
             at = pl.ds(pl.multiple_of(r * 32, 32), 32)
-            sent[slot, at, :] = (
-                sent[slot, at, :].astype(F32) + got[slot, at, :].astype(F32)
-            ).astype(BF)
+            dst[:, at, :] = (dst[:, at, :].astype(F32) + src[:, at, :].astype(F32)).astype(BF)
             return c
 
         lax.fori_loop(0, rows // 32, add, 0)
@@ -539,7 +490,21 @@
 
     def step(i, c):
         goal = jnp.where(i == 0, far_outer, jnp.where(i == 1, far_inner, jnp.where(i == 2, near, z)))
-        block(i, goal)
+        attend_rows(goal)
+
+        @pl.when(i == 0)
+        def _():
+            for kind in (1, 2, 4):
+                ow_wait(kind)
+
+        dst = slab(i)
+        for t in range(4):
+            dst[t] = jnp.dot(att[...], ow_all[t], preferred_element_type=F32).astype(BF)
+
+        @pl.when(i == 0)
+        def _():
+            pl.semaphore_wait(ready, 3)
+
         for slot in range(2):
             @pl.when(jnp.logical_not(inner) & (i == slot))
             def _():
@@ -561,40 +526,67 @@
 
     lax.fori_loop(0, 4, step, 0)
     to_near[2].wait_recv()
-    copy(0, 3, far_outer).wait_recv()
+    send(0, 3, far_outer).wait_recv()
+    own, direct, summed = slab(3), slab(6), slab(7)
+
+    def finish(r, c):
+        at = pl.ds(pl.multiple_of(r * 32, 32), 32)
+        for t in range(4):
+            cols = slice(t * width, (t + 1) * width)
+            total = own[t, at, :].astype(F32)
+            total = total + direct[t, at, :].astype(F32)
+            total = total + summed[t, at, :].astype(F32)
+            o_ref[at, cols] = (
+                lat_ref[at, cols].astype(F32) + mod_out[2:3, cols] * total
+            ).astype(BF)
+        return c
+
+    lax.fori_loop(0, rows // 32, finish, 0)
     for slot in range(3):
         to_near[slot].wait_send()
-
-    def finish(r, c):
-        at = pl.ds(pl.multiple_of(r * 32, 32), 32)
-        total = sent[3, at, :].astype(F32)
-        total = total + got[2, at, :].astype(F32)
-        total = total + got[3, at, :].astype(F32)
-        o_ref[at, :] = (lat_ref[at, :].astype(F32) + mod_ref[2:3, :] * total).astype(BF)
-        return c
-
-    lax.fori_loop(0, rows // 32, finish, 0)
-
-
-def attend_out(q, kv, bias, ow_all, latents, mod_full):
+    for i in range(4):
+        @pl.when(s < 3)
+        def _():
+            kv_copy(0, i, shard_of(i)).wait_send()
+
+        @pl.when(s > 0)
+        def _():
+            kv_copy(1, i, shard_of(i)).wait_send()
+    for step_id in range(1, 16):
+        mod_copy(step_id).wait_send()
+    for kind in range(5):
+        ow_copy(kind).wait_send()
+
+
+def whole_block(latents, w, ow, mod, q_gain, k_gain, bias):
+    rows, model = latents.shape
+    width = w.shape[1]
     vmem = pl.BlockSpec(memory_space=pltpu.VMEM)
-    rows, model = latents.shape
+    place = pl.BlockSpec(memory_space=pl.ANY)
+    dma = pltpu.SemaphoreType.DMA
     return pl.pallas_call(
-        attend_out_kernel,
+        block_kernel,
         out_shape=jax.ShapeDtypeStruct(latents.shape, BF),
-        in_specs=[vmem] * 6,
+        in_specs=[vmem, place, place, vmem, vmem, vmem, vmem],
         out_specs=vmem,
         scratch_shapes=[
-            pltpu.VMEM((rows, q.shape[1]), BF),
+            pltpu.VMEM((4 * rows, width), BF),
+            pltpu.VMEM((3, 4 * rows, 2 * width), BF),
+            pltpu.VMEM((4,) + ow.shape, BF),
+            pltpu.VMEM((8, model), F32),
             pltpu.VMEM((4, rows, model), BF),
-            pltpu.VMEM((4, rows, model), BF),
-            pltpu.SemaphoreType.DMA((4,)),
-            pltpu.SemaphoreType.DMA((4,)),
+            pltpu.VMEM((3, 4) + w.shape[1:], BF),
+            pltpu.VMEM((16,) + mod.shape, F32),
+            pltpu.VMEM((rows, model), BF),
+            pltpu.VMEM((rows, width), BF),
+            dma((6,)), dma((15,)), dma((15,)), dma((2, 3)), dma((2, 3)),
+            dma((3, 5)), dma((3, 5)), dma((5,)), dma((5,)), dma((2, 4)), dma((2, 4)),
+            dma((4,)), dma((4,)), pltpu.SemaphoreType.REGULAR,
         ],
         compiler_params=pltpu.CompilerParams(
-            collective_id=1, has_side_effects=True, vmem_limit_bytes=VMEM_LIMIT
+            collective_id=0, has_side_effects=True, vmem_limit_bytes=VMEM_LIMIT
         ),
-    )(q, kv, bias, ow_all, latents, mod_full)
+    )(latents, w, ow, mod, q_gain, k_gain, bias)
 
 
 def key_bias(tile_slot, win_start, block_idx):
@@ -631,10 +623,7 @@
     own_mod = jnp.pad(own_mod, ((0, 5), (0, 0)))
     w = jnp.transpose(qkv_weight, (1, 0, 2))
     bias = key_bias(tile_slot, win_start, lax.axis_index("seq"))
-    q, kv, ow_all, mod_full = gather_project(
-        latents, w, out_weight, own_mod, q_gain[None], k_gain[None]
-    )
-    return attend_out(q, kv, bias, ow_all, latents, mod_full)
+    return whole_block(latents, w, out_weight, own_mod, q_gain[None], k_gain[None], bias)
 
 
 def solution(mesh):

time: 261 us -> 246 us (0.943)
  Pallas kernels: 253 us -> 238 us
    pallas_call x2 -> x1, Pallas kernels: 253 us -> 238 us  [whole_block(): pl.pallas_call(block_kernel, out_shape=jax.ShapeDtypeStruct(latents.shape...]
where the time goes in v4:
time: 246 us
  Pallas kernels  238 us (97%)
  local copies, waits for them, and re-layouts  5.08 us (2%)
    pallas_call x1, Pallas kernels, whole_block(): pl.pallas_call(block_kernel, out_shape=jax.ShapeDtypeStruct(latents.shape...  238 us

profile of v4, /device:TPU:9, one launch (start us, length us, event | category | flops | bytes accessed | tf_op | source)
XLA Modules:
  0.0 245.7 jit_solution(7094200459467719296)
XLA Ops:
  0.0 0.0 copy-start
  0.8 0.7 constant_dynamic-slice_fusion.3
  1.5 0.8 fusion.7
  2.4 0.1 iota_compare_fusion
  2.4 0.1 select_reduce_fusion
  2.6 0.1 compare_and_fusion.2
  2.7 0.1 add_select_fusion
  2.8 0.0 copy-done
  2.8 0.2 fusion
  3.0 0.6 pad.4.mod_ref
  3.6 0.2 broadcast_in_dim.58
  3.8 0.9 broadcast_in_dim_reshape.3.bias_ref
  4.7 238.3 %shard_map.91 = bf16[256,3072]{1,0:T(8,128)(2,1)} custom-call(bf16[256,3072]{1,0:T(8,128)(2,1)} %lat_ref.1, bf16[3,768,768]{2,1,0:T(8,128)(2,1)} %bitcast.46, bf16[768,768]{1,0:T(8,128)(2,1)} %ow_ref.1, f32[8,192]{1,0:T(8,128)} %pad.4.mod_ref, f32[1,128]{1,0:T(1,128)} %bitcast.49, f32[1,128]{1,0:T(1,128)} %bitcast.50, ...), custom_call_target="tpu_custom_call" | custom-call | tf_op jit(solution)/shard_map/pallas_call | solution.py:567
  243.0 2.7 %copy.20 = bf16[256,3072]{1,0:T(8,128)(2,1)} copy(bf16[256,3072]{1,0:T(8,128)(2,1)} %shard_map.91) | data formatting | bytes 3145728
  (9 shorter events, 0.1 us)
Async XLA Ops:
  0.0 2.8 %copy-start = (bf16[256,3,192]{0,2,1:T(8,128)(2,1)S(1)}, bf16[256,3,192]{0,2,1:T(8,128)(2,1)}, u32[]{:S(2)}) copy-start(bf16[256,3,192]{0,2,1:T(8,128)(2,1)} %param.12) | copy-start | bytes 884740
